TPU v7x, 32 devices: a whole 2x2x4 slice. The times are simulated.
32 devices in a mesh: groups: 2 (over y), ep: 8 (over z, x), tp: 2 (over core).
Axes of the slice: x: 2, y: 2, z: 4, core: 2. Of those that a mesh axis runs over, the one named last changes fastest.
Arguments:
- tokens: bfloat16 [1024, 2880], P(('groups', 'ep'), 'tp'), parts along dimension 0, may hold values from -6 to 6
- expert_ids: int32 [1024, 4], P(('groups', 'ep')), parts along dimension 0, may hold values from 0 to 7, all different within a row; in each aligned block of 64 rows (0 to 63, 64 to 127, ...) at most 48 rows name the same one
- gate_probs: float32 [1024, 4], P(('groups', 'ep')), parts along dimension 0, may hold values from 0.05 to 1
- w_gate: bfloat16 [8, 2880, 1440], P('ep', None, 'tp'), may hold values from -0.109375 to 0.109375
- w_up: bfloat16 [8, 2880, 1440], P('ep', None, 'tp'), may hold values from -0.109375 to 0.109375
- w_down: bfloat16 [8, 1440, 2880], P('ep', 'tp'), may hold values from -0.15625 to 0.15625
Outputs:
- mixed: bfloat16 [1024, 2880], P(('groups', 'ep'), 'tp'), parts along dimension 0
There are 2 independent parts, one for each index of `groups`. A program takes and returns all parts, laid end to end along the dimension named above; an argument that names none is the same for every part. Nothing has to cross between parts.
Inputs may be any that keep to these rules, and one draw needn't show every extreme that they name: `expert_ids`: within each block of 64 rows that one index of ep holds, no expert is named by more than 48 rows, and in every draw some expert is named by exactly 48 rows of some block; the numbers of one row differ.
All inputs are finite; a program needn't handle non-finite values.
Results may differ from a plain program's by a relative error of at most 0.0058.
Values may be sent and summed in bfloat16 or wider, within the bound.
A program may use at most 128 MiB of HBM per device.

v0:
```python
import jax
import jax.numpy as jnp
from jax import lax
from jax.sharding import PartitionSpec as P


def swiglu_expert(rows, gate_part, up_part, down_part):
    gated = jnp.dot(rows, gate_part, preferred_element_type=jnp.float32)
    lifted = jnp.dot(rows, up_part, preferred_element_type=jnp.float32)
    hidden = (jax.nn.silu(gated) * lifted).astype(jnp.bfloat16)
    return jnp.dot(hidden, down_part, preferred_element_type=jnp.float32)


def slot_table(expert_ids, n_experts):
    routed = expert_ids.reshape(-1)
    pair_count = routed.shape[0]
    onehot = (routed[:, None] == jnp.arange(n_experts, dtype=jnp.int32)[None, :]).astype(
        jnp.bfloat16
    )
    row_index = lax.broadcasted_iota(jnp.int32, (pair_count, pair_count), 0)
    col_index = lax.broadcasted_iota(jnp.int32, (pair_count, pair_count), 1)
    earlier = (row_index > col_index).astype(jnp.bfloat16)
    before = jnp.dot(earlier, onehot, preferred_element_type=jnp.float32)
    slots = jnp.sum(before * onehot.astype(jnp.float32), axis=1).astype(jnp.int32)
    return (routed, slots)


def body(tokens, expert_ids, gate_probs, w_gate, w_up, w_down):
    n_experts = lax.axis_size("ep")
    tok_rows, top_count = expert_ids.shape
    capacity = 3 * tok_rows * top_count // (2 * n_experts)
    routed, slots = slot_table(expert_ids, n_experts)
    positions = routed * capacity + slots
    pair_token = jnp.repeat(jnp.arange(tok_rows, dtype=jnp.int32), top_count)
    buffer_rows = n_experts * capacity
    owners = jnp.full((buffer_rows,), tok_rows, jnp.int32).at[positions].set(pair_token)
    half_slots = capacity // 2
    whole_tokens = lax.all_gather(tokens, "tp", axis=1, tiled=True)
    width = whole_tokens.shape[1]
    gate_full, up_full = (
        lax.all_gather(w_gate, "tp", axis=2, tiled=True),
        lax.all_gather(w_up, "tp", axis=2, tiled=True),
    )
    down_full = lax.all_gather(w_down, "tp", axis=1, tiled=True)
    padded = jnp.concatenate([whole_tokens, jnp.zeros((1, width), whole_tokens.dtype)], 0)
    outgoing = padded[owners].reshape(n_experts, capacity, width)
    lane = lax.axis_index("tp")
    mine = lax.dynamic_slice_in_dim(outgoing, lane * half_slots, half_slots, 1)
    block = lax.all_to_all(mine, "ep", split_axis=0, concat_axis=0, tiled=True)
    sources, items, columns = block.shape
    result = swiglu_expert(
        block.reshape(sources * items, columns), gate_full[0], up_full[0], down_full[0]
    )
    result = result.astype(jnp.bfloat16).reshape(sources, items, columns)
    returned = lax.all_to_all(result, "ep", split_axis=0, concat_axis=0, tiled=True)
    received = returned.reshape(n_experts * half_slots, width)
    in_half = slots // half_slots == lane
    local_pos = routed * half_slots + slots % half_slots
    picked = received[local_pos].astype(jnp.float32).reshape(tok_rows, top_count, width)
    weighted = jnp.where(in_half.reshape(tok_rows, top_count), gate_probs, 0.0)
    partial_value = jnp.sum(weighted[:, :, None] * picked, axis=1)
    return lax.psum_scatter(partial_value, "tp", scatter_dimension=1, tiled=True).astype(
        jnp.bfloat16
    )


def solution(mesh):
    in_specs = (
        P(("groups", "ep"), "tp"),
        P(("groups", "ep"), None),
        P(("groups", "ep"), None),
        P("ep", None, "tp"),
        P("ep", None, "tp"),
        P("ep", "tp", None),
    )
    out_specs = P(("groups", "ep"), "tp")
    return jax.shard_map(body, mesh=mesh, in_specs=in_specs, out_specs=out_specs, check_vma=False)
```

profile of v0, /device:TPU:9, one launch (start us, length us, event | category | flops | bytes accessed | tf_op | source)
XLA Modules:
  0.0 151.6 jit_solution(289677251777825991)
XLA Ops:
  6.5 0.7 all-gather.5.cloned.1.call-update
  7.3 0.7 all-gather.7.cloned.1.call-update
  8.1 0.7 all-gather.9.cloned.1.call-update
  8.8 0.1 copy.23
  8.9 0.1 eq.24
  9.0 0.2 fusion.15
  9.2 0.1 copy.29
  9.3 0.1 mul.55
  9.4 0.1 copy.30
  9.5 0.1 mul.60
  9.6 0.1 reshape.139
  9.7 2.4 %all-gather = bf16[2,1440,64]{1,2,0:T(8,128)(2,1)S(1)} all-gather(bf16[1,1440,64]{1,2,0:T(8,128)(2,1)S(1)} %bitcast.41), channel_id=1, replica_groups=mesh['groups'=2,'ep'=8,'tp'=2] {'tp'}, dimensions={0}, use_global_device_ids=true | all-gather | bytes 552960 | tf_op jit(solution)/shard_map/all_gather | solution.py:38
  12.1 0.4 copy.28
  12.5 0.3 reshape.145
  12.9 1.4 scatter_custom_fusion
  14.3 2.9 %gather_fusion = bf16[384,2880]{1,0:T(8,128)(2,1)S(1)} fusion(bf16[65,2880]{1,0:T(8,128)(2,1)S(1)} %concatenate.3, s32[1024]{0:T(1024)S(1)} %pad_clamp_fusion.1), kind=kCustom, calls=%fused_computation | custom fusion | bytes 4425216 | tf_op jit(solution)/shard_map/gather | solution.py:46
  17.2 0.1 constant_dynamic-slice_fusion
  17.3 32.0 %all_to_all.10 = bf16[8,24,2880]{2,1,0:T(8,128)(2,1)S(1)} all-to-all(bf16[8,24,2880]{2,1,0:T(8,128)(2,1)S(1)} %constant_dynamic-slice_fusion), channel_id=1, replica_groups=mesh['groups'=2,'ep'=8,'tp'=2] {'ep'}, dimensions={0} | all-to-all | bytes 2211840 | tf_op jit(solution)/shard_map/all_to_all | solution.py:49
  49.4 6.2 %fusion.4 = f32[192,1440]{1,0:T(8,128)S(1)} fusion(bf16[192,2880]{1,0:T(8,128)(2,1)S(1)} %bitcast.38, bf16[1,2880,1440]{1,2,0:T(8,128)(2,1)} %all-gather.5.cloned.1.call-done), kind=kOutput, calls=%fused_computation.7 | convolution fusion | flops 1592524800 | bytes 10506240 | tf_op jit(solution)/shard_map/dot_general | solution.py:8
  55.6 22.8 %all-gather.9.cloned.1.call-done = bf16[1,1440,2880]{2,1,0:T(8,128)(2,1)} async-done(((bf16[1,720,2880]{2,1,0:T(8,128)(2,1)}), bf16[1,1440,2880]{2,1,0:T(8,128)(2,1)}) %all-gather.9.cloned.1.call-update) | async-done | bytes 8294416 | tf_op jit(solution)/shard_map/all_gather | solution.py:44
  78.4 11.6 %fusion.6 = bf16[192,2880]{1,0:T(8,128)(2,1)} fusion(bf16[1,1440,2880]{2,1,0:T(8,128)(2,1)} %all-gather.9.cloned.1.call-done, bf16[192,2880]{1,0:T(8,128)(2,1)S(1)} %bitcast.39, bf16[1,2880,1440]{1,2,0:T(8,128)(2,1)} %all-gather.7.cloned.1.call-done, f32[192,1440]{1,0:T(8,128)S(1)} %fusion.4), kind=kOutput, calls=%fused_computation.9 | convolution fusion | flops 3187261440 | bytes 19906560 | tf_op jit(solution)/shard_map/dot_general | solution.py:11
  90.0 5.6 %all-to-all-start.1 = ((bf16[8,24,2880]{2,1,0:T(8,128)(2,1)}), bf16[8,24,2880]{2,1,0:T(8,128)(2,1)S(1)}, u32[]{:S(2)}, u32[]{:S(2)}) async-start(bf16[8,24,2880]{2,1,0:T(8,128)(2,1)} %bitcast.10), calls=%async_computation.1 | async-start | bytes 2260992 | tf_op jit(solution)/shard_map/all_to_all | solution.py:55
  95.7 0.1 div.15
  95.9 0.1 and.21
  96.1 0.1 copy.27
  96.2 24.9 %all-to-all-done.1 = bf16[8,24,2880]{2,1,0:T(8,128)(2,1)S(1)} async-done(((bf16[8,24,2880]{2,1,0:T(8,128)(2,1)}), bf16[8,24,2880]{2,1,0:T(8,128)(2,1)S(1)}, u32[]{:S(2)}, u32[]{:S(2)}) %all-to-all-start.1) | async-done | bytes 1105952 | tf_op jit(solution)/shard_map/all_to_all | solution.py:55
  121.1 2.7 %gather_fusion.1 = bf16[256,2880]{1,0:T(8,128)(2,1)} fusion(bf16[192,2880]{1,0:T(8,128)(2,1)S(1)} %bitcast.34, s32[1024]{0:T(1024)S(1)} %pad_clamp_fusion), kind=kCustom, calls=%fused_computation.1 | custom fusion | bytes 2950144 | tf_op jit(solution)/shard_map/gather | solution.py:59
  123.8 2.8 %reshape.118 = f32[64,4,2880]{2,1,0:T(4,128)S(1)} reshape(bf16[256,2880]{1,0:T(8,128)(2,1)} %gather_fusion.1) | data formatting | bytes 4423680 | tf_op jit(solution)/shard_map/convert_element_type | solution.py:59
  126.6 2.9 %multiply_reduce_fusion = f32[64,2880]{1,0:T(8,128)} fusion(f32[64,4,2880]{2,1,0:T(4,128)S(1)} %reshape.118, f32[64,4]{1,0:T(8,128)S(1)} %copy.27), kind=kLoop, calls=%fused_computation.10 | loop fusion | flops 1290240 | bytes 3687424 | tf_op jit(solution)/shard_map/reduce_sum | solution.py:61
  129.5 2.7 %copy.31 = f32[64,2880]{0,1:T(8,128)} copy(f32[64,2880]{1,0:T(8,128)} %multiply_reduce_fusion) | data formatting | bytes 1474560
  132.2 10.9 %reduce-scatter.4.cloned.1.call-done = f32[1440,64]{1,0:T(8,128)} async-done(((f32[2880,64]{1,0:T(8,128)}), f32[1440,64]{1,0:T(8,128)}) %reduce-scatter.4.cloned.1.call-update) | async-done | bytes 368656
  143.1 1.9 %copy.32 = bf16[64,1440]{1,0:T(8,128)(2,1)} copy(f32[64,1440]{0,1:T(8,128)} %bitcast.40) | data formatting | bytes 552960
  (26 shorter events, 0.4 us)
Async XLA Ops:
  6.5 42.8 %all-gather.5.cloned.1.call-start = ((), (), s32[]{:S(2)}) async-start(), calls=%async_computation.3 | async-start | bytes 12718080 | tf_op jit(solution)/shard_map/all_gather | solution.py:41
  7.3 48.3 %all-gather.7.cloned.1.call-start = ((), (), s32[]{:S(2)}) async-start(), calls=%async_computation.4 | async-start | bytes 12718080 | tf_op jit(solution)/shard_map/all_gather | solution.py:42
  8.0 0.8 copy-start.1
  8.0 1.7 %copy-start = (bf16[64,1440]{1,0:T(8,128)(2,1)S(1)}, bf16[64,1440]{1,0:T(8,128)(2,1)}, u32[]{:S(2)}) copy-start(bf16[64,1440]{1,0:T(8,128)(2,1)} %param.6) | copy-start | bytes 552964
  8.0 70.4 %all-gather.9.cloned.1.call-start = ((), (), s32[]{:S(2)}) async-start(), calls=%async_computation.5 | async-start | bytes 12718080 | tf_op jit(solution)/shard_map/all_gather | solution.py:44
  90.0 6.1 %copy-start.2 = (f32[64,4]{0,1:T(4,128)S(1)}, f32[64,4]{0,1:T(4,128)}, u32[]{:S(2)}) copy-start(f32[64,4]{0,1:T(4,128)} %param.8) | copy-start | bytes 3076
  90.0 31.1 %all-to-all-start.1 = ((bf16[8,24,2880]{2,1,0:T(8,128)(2,1)}), bf16[8,24,2880]{2,1,0:T(8,128)(2,1)S(1)}, u32[]{:S(2)}, u32[]{:S(2)}) async-start(bf16[8,24,2880]{2,1,0:T(8,128)(2,1)} %bitcast.10), calls=%async_computation.1 | async-start | bytes 2260992 | tf_op jit(solution)/shard_map/all_to_all | solution.py:55
  95.6 47.5 %reduce-scatter.4.cloned.1.call-start = ((), (), s32[]{:S(2)}) async-start(), calls=%async_computation.6 | async-start | bytes 2211840
Sparse Core Ops, SparseCore 0:
  8.9 22.5 all-gather.4
  33.1 21.8 all-gather.6
  56.5 21.8 all-gather.8
  132.4 10.6 reduce-scatter.3
where the time goes:
time: 153 us; the launch traced here: 152 us
  waiting for transfers between devices  60.7 us (40%)
  blocking collectives  34.4 us (22%)
  matrix products  18 us (12%)
  local copies, waits for them, and re-layouts  16.4 us (11%)
  between operations  13.3 us (9%)
  starting transfers between devices  5.7 us (4%)
  other arithmetic  2.99 us (2%)
    all_to_all x1, blocking collectives, body(): block = lax.all_to_all(mine, 'ep', split_axis=0, concat_axis=0, tiled=True)  32 us
    all_to_all x1, waiting for transfers between devices, body(): lax.all_to_all(result, 'ep', split_axis=0, concat_axis=0, tiled=True)  24.9 us
    all_gather x1, waiting for transfers between devices, body(): down_full = lax.all_gather(w_down, 'tp', axis=1, tiled=True)  22.8 us
    unnamed x5, waiting for transfers between devices  13 us
    dot_general x1, matrix products, swiglu_expert(): return jnp.dot(hidden, down_part, preferred_element_type=jnp.float32)  11.6 us
    dot_general x1, matrix products, swiglu_expert(): gated = jnp.dot(rows, gate_part, preferred_element_type=jnp.float32)  6.2 us
    all_to_all x1, starting transfers between devices, body(): lax.all_to_all(result, 'ep', split_axis=0, concat_axis=0, tiled=True)  5.62 us
    unnamed x10, local copies, waits for them, and re-layouts  5.07 us
  transfers between devices with their start and end apart: 5, of which 3 were waited for; matrix products, arithmetic and copies ran while one was open for 8% of the time, Pallas kernels for 0%

commit v1 on v0

--- a/solution.py
+++ b/solution.py
@@ -64,6 +64,23 @@
     )
 
 
+def dense_body(tokens, expert_ids, gate_probs, w_gate, w_up, w_down):
+    n_experts = lax.axis_size("ep")
+    tok_rows, _ = expert_ids.shape
+    experts = jnp.arange(n_experts, dtype=jnp.int32)
+    match = expert_ids[:, :, None] == experts[None, None, :]
+    weight = jnp.sum(jnp.where(match, gate_probs[:, :, None], 0.0), axis=1)
+    weights = lax.all_gather(weight, "ep", axis=0, tiled=True)
+    mine = (experts == lax.axis_index("ep"))[None, :]
+    column = jnp.sum(jnp.where(mine, weights, 0.0), axis=1, keepdims=True)
+    rows = lax.all_gather(tokens, "tp", axis=1, tiled=True)
+    rows = lax.all_gather(rows, "ep", axis=0, tiled=True)
+    result = swiglu_expert(rows, w_gate[0], w_up[0], w_down[0]) * column
+    result = lax.psum_scatter(result.astype(jnp.bfloat16), "tp", scatter_dimension=1, tiled=True)
+    result = lax.psum_scatter(result, "ep", scatter_dimension=0, tiled=True)
+    return result.astype(jnp.bfloat16)
+
+
 def solution(mesh):
     in_specs = (
         P(("groups", "ep"), "tp"),
@@ -74,4 +91,12 @@
         P("ep", "tp", None),
     )
     out_specs = P(("groups", "ep"), "tp")
-    return jax.shard_map(body, mesh=mesh, in_specs=in_specs, out_specs=out_specs, check_vma=False)
+
+    def layer(tokens, expert_ids, gate_probs, w_gate, w_up, w_down):
+        n_experts = lax.axis_size("ep")
+        tok_rows, top_count = expert_ids.shape
+        capacity = 3 * tok_rows * top_count // (2 * n_experts)
+        chosen = dense_body if tok_rows <= 2 * capacity else body
+        return chosen(tokens, expert_ids, gate_probs, w_gate, w_up, w_down)
+
+    return jax.shard_map(layer, mesh=mesh, in_specs=in_specs, out_specs=out_specs, check_vma=False)

time: 153 us -> 176 us (1.15)
  the two profiles are of different devices: /device:TPU:9 before, /device:TPU:0 now
where the time goes in v1:
time: 176 us
  waiting for transfers between devices  105 us (60%)
  blocking collectives  34.9 us (20%)
  matrix products  17.3 us (10%)
  between operations  13.1 us (7%)
  local copies, waits for them, and re-layouts  4.13 us (2%)
    reduce_scatter x1, waiting for transfers between devices, dense_body(): result = lax.psum_scatter(result, 'ep', scatter_dimension=0, tiled=True)  67.7 us
    all_gather x1, blocking collectives, dense_body(): weights = lax.all_gather(weight, 'ep', axis=0, tiled=True)  32.5 us
    all_gather x1, waiting for transfers between devices, dense_body(): rows = lax.all_gather(rows, 'ep', axis=0, tiled=True)  27.9 us
    dot_general x1, matrix products, swiglu_expert(): return jnp.dot(hidden, down_part, preferred_element_type=jnp.float32)  10.4 us
    reduce_scatter x1, waiting for transfers between devices, dense_body(): lax.psum_scatter(result.astype(jnp.bfloat16), 'tp', scatter_dimension=1,...  9.69 us
    dot_general x1, matrix products, swiglu_expert(): gated = jnp.dot(rows, gate_part, preferred_element_type=jnp.float32)  6.87 us
    unnamed x5, local copies, waits for them, and re-layouts  3.72 us
  transfers between devices with their start and end apart: 3, of which 3 were waited for; matrix products, arithmetic and copies ran while one was open for 1% of the time, Pallas kernels for 0%

profile of v1, /device:TPU:0, one launch (start us, length us, event | category | flops | bytes accessed | tf_op | source)
XLA Modules:
  0.0 175.7 jit_solution(2186154354982800531)
XLA Ops:
  6.5 0.0 all-gather.4.cloned.1.call-start
  6.5 2.4 %all-gather = bf16[2,1440,64]{1,2,0:T(8,128)(2,1)S(1)} all-gather(bf16[1,1440,64]{1,2,0:T(8,128)(2,1)} %bitcast.26), channel_id=1, replica_groups=mesh['groups'=2,'ep'=8,'tp'=2] {'tp'}, dimensions={0}, use_global_device_ids=true | all-gather | bytes 552960 | tf_op jit(solution)/shard_map/all_gather | solution.py:76
  8.9 0.4 copy.23
  9.4 1.1 reshape.8
  10.4 0.0 all-gather.4.cloned.1.call-update
  10.4 0.0 reduce-scatter.5.cloned.1.call-start
  10.5 0.7 select_reduce_fusion.1
  11.2 32.5 %all-gather.1 = f32[8,64,8]{1,2,0:T(8,128)S(1)} all-gather(f32[1,64,8]{1,2,0:T(8,128)S(1)} %bitcast.27), channel_id=1, replica_groups=mesh['groups'=2,'ep'=8,'tp'=2] {'ep'}, dimensions={0}, use_global_device_ids=true | all-gather | bytes 18432 | tf_op jit(solution)/shard_map/all_gather | solution.py:73
  43.8 0.1 reshape.10
  43.8 0.1 select_reduce_fusion
  43.9 27.9 %all-gather.4.cloned.1.call-done = bf16[512,2880]{1,0:T(8,128)(2,1)} async-done(((bf16[64,2880]{1,0:T(8,128)(2,1)}), bf16[512,2880]{1,0:T(8,128)(2,1)}) %all-gather.4.cloned.1.call-update) | async-done | bytes 2949136 | tf_op jit(solution)/shard_map/all_gather | solution.py:77
  71.8 0.0 copy-start
  71.8 6.9 %fusion.3 = f32[512,720]{0,1:T(8,128)} fusion(bf16[512,2880]{1,0:T(8,128)(2,1)} %all-gather.4.cloned.1.call-done, bf16[1,2880,720]{1,2,0:T(8,128)(2,1)} %param.9), kind=kOutput, calls=%fused_computation.4 | convolution fusion | flops 2123366400 | bytes 8570880 | tf_op jit(solution)/shard_map/dot_general | solution.py:8
  78.7 0.0 copy-done
  78.7 10.4 %multiply_convert_fusion = bf16[512,2880]{0,1:T(8,128)(2,1)} fusion(bf16[1,720,2880]{2,1,0:T(8,128)(2,1)} %param.11, f32[512]{0:T(512)S(1)} %select_reduce_fusion, f32[512,720]{0,1:T(8,128)} %fusion.3, bf16[512,2880]{1,0:T(8,128)(2,1)S(1)} %copy-done, bf16[1,2880,720]{1,2,0:T(8,128)(2,1)} %param.10), kind=kOutput, calls=%fused_computation | convolution fusion | flops 4251893760 | bytes 15669248 | tf_op jit(solution)/shard_map/dot_general | solution.py:11
  89.1 0.0 reduce-scatter.5.cloned.1.call-update
  89.1 0.0 reduce-scatter.7.cloned.1.call-start
  89.2 9.7 %reduce-scatter.5.cloned.1.call-done = bf16[512,1440]{0,1:T(8,128)(2,1)} async-done(((bf16[512,2880]{0,1:T(8,128)(2,1)}), bf16[512,1440]{0,1:T(8,128)(2,1)}) %reduce-scatter.5.cloned.1.call-update) | async-done | bytes 1474576 | tf_op jit(solution)/shard_map/reduce_scatter | solution.py:79
  98.9 2.6 %copy.26 = bf16[512,1440]{1,0:T(8,128)(2,1)} copy(bf16[512,1440]{0,1:T(8,128)(2,1)} %reduce-scatter.5.cloned.1.call-done) | data formatting | bytes 2949120
  101.5 0.0 reduce-scatter.7.cloned.1.call-update
  101.5 67.7 %reduce-scatter.7.cloned.1.call-done = bf16[64,1440]{1,0:T(8,128)(2,1)} async-done(((bf16[512,1440]{1,0:T(8,128)(2,1)}), bf16[64,1440]{1,0:T(8,128)(2,1)}) %reduce-scatter.7.cloned.1.call-update) | async-done | bytes 184336 | tf_op jit(solution)/shard_map/reduce_scatter | solution.py:80
  (2 shorter events, 0.0 us)
Async XLA Ops:
  6.5 65.3 %all-gather.4.cloned.1.call-start = ((), (), s32[]{:S(2)}) async-start(), calls=%async_computation.2 | async-start | bytes 3391488 | tf_op jit(solution)/shard_map/all_gather | solution.py:77
  10.4 88.4 %reduce-scatter.5.cloned.1.call-start = ((), (), s32[]{:S(2)}) async-start(), calls=%async_computation.3 | async-start | bytes 4423680 | tf_op jit(solution)/shard_map/reduce_scatter | solution.py:79
  71.8 6.9 %copy-start = (bf16[512,2880]{1,0:T(8,128)(2,1)S(1)}, bf16[512,2880]{1,0:T(8,128)(2,1)}, u32[]{:S(2)}) copy-start(bf16[512,2880]{1,0:T(8,128)(2,1)} %all-gather.4.cloned.1.call-done) | copy-start | bytes 8847364
  89.1 80.1 %reduce-scatter.7.cloned.1.call-start = ((), (), s32[]{:S(2)}) async-start(), calls=%async_computation.4 | async-start | bytes 1769472 | tf_op jit(solution)/shard_map/reduce_scatter | solution.py:80
Sparse Core Ops, SparseCore 0:
  10.6 61.2 all-gather.3
  89.3 9.5 reduce-scatter.4
  102.3 66.8 reduce-scatter.6
